TPU v7x, 128 devices: a whole 4x4x4 slice. The times are simulated.
128 devices in a mesh: req: 16 (over z, y), mp: 8 (over x, core).
Axes of the slice: x: 4, y: 4, z: 4, core: 2. Of those that a mesh axis runs over, the one named last changes fastest.
Arguments:
- q_pre: bfloat16 [8192, 3072], P('req', 'mp'), may hold values from -64 to 64
- k_pre: bfloat16 [8192, 1024], P('req', 'mp'), may hold values from -64 to 64
- v_pre: bfloat16 [8192, 1024], P('req', 'mp'), may hold values from -12 to 12
- q_bias: float32 [3072], P('mp'), may hold values from -3 to 3
- k_bias: float32 [1024], P('mp'), may hold values from -3 to 3
- v_bias: float32 [1024], P('mp'), may hold values from -3 to 3
- segment_ids: int32 [8192], P('req'), may hold values from -1 to 63, as said below
- lengths: int32 [16, 4], replicated, may hold values from 64 to 128, as said below
- page_table: int32 [16, 4], replicated, may hold values from 0 to 63, as said below
- w_out: bfloat16 [3072, 5120], P('mp'), may hold values from -0.109375 to 0.109375
- residual: bfloat16 [8192, 5120], P('req'), may hold values from -4 to 4
- norm_gain: float32 [5120], replicated, may hold values from 0.1 to 1.9
- w_gate: bfloat16 [5120, 6912], P('req', 'mp'), may hold values from -0.078125 to 0.078125
- w_up: bfloat16 [5120, 6912], P('req', 'mp'), may hold values from -0.078125 to 0.078125
Outputs:
- hidden: bfloat16 [8192, 6912], P('req', 'mp')
- kv_cache: bfloat16 [64, 8, 128, 256], P('req', 'mp')
Inputs may be any that keep to these rules, and one draw needn't show every extreme that they name: Requests of block r lie in order from the block's first token, request j taking lengths[r, j] tokens; in every block one request has exactly 128 tokens. `segment_ids`: token t of block r carries r * 4 + j inside request j's run of tokens given by lengths, and -1 after the last request of its block. `page_table`: every page is named once; page p is held by req index p // 4; the requests of one block have pages held by different req indices.
All inputs are finite; a program needn't handle non-finite values.
Results may differ from a plain program's by a relative error of at most 0.019.
Values may be sent and summed in bfloat16 or wider, within the bound.
A program may use at most 128 MiB of HBM per device.

v0:
```python
import math
import jax
import jax.numpy as jnp
from jax import lax
from jax.sharding import PartitionSpec as P

HD = 128
PAGE = 128
REQS = 4
THETA = 1000000.0
EPS = 1e-06


def rotate(values, positions):
    half_dim = values.shape[-1] // 2
    frequencies = THETA ** (-jnp.arange(half_dim, dtype=jnp.float32) * (2.0 / values.shape[-1]))
    angles = positions[:, None] * frequencies[None, :]
    cosine = jnp.cos(angles)[:, None, :]
    sine_part = jnp.sin(angles)[:, None, :]
    first_half = values[..., :half_dim]
    second = values[..., half_dim:]
    return jnp.concatenate(
        [first_half * cosine - second * sine_part, second * cosine + first_half * sine_part],
        axis=-1,
    )


def attend(queries, keys, values, length):
    scale_factor = 1.0 / math.sqrt(queries.shape[-1])
    scores = (
        jnp.einsum("sqhge,skhe->shgqk", queries, keys, preferred_element_type=jnp.float32)
        * scale_factor
    )
    page_len = queries.shape[1]
    query_pos = jnp.arange(page_len)[:, None]
    key_pos = jnp.arange(page_len)[None, :]
    allowed = (key_pos <= query_pos)[None] & (key_pos[None] < length[:, None, None])
    allowed = allowed[:, None, None]
    row_max = jnp.max(jnp.where(allowed, scores, -1e30), axis=-1, keepdims=True)
    weights = jnp.where(allowed, jnp.exp(scores - row_max), 0.0)
    row_sum = jnp.sum(weights, axis=-1, keepdims=True)
    present = (jnp.arange(page_len)[None, :] < length[:, None])[:, None, None, :, None]
    row_probs = jnp.where(present, weights / jnp.where(present, row_sum, 1.0), 0.0).astype(
        jnp.bfloat16
    )
    mixed_rows = jnp.einsum(
        "shgqk,skhe->sqhge", row_probs, values, preferred_element_type=jnp.float32
    )
    return mixed_rows.astype(jnp.bfloat16)


def normalize(resid_rows, summed, gain_row):
    state = resid_rows.astype(jnp.float32) + summed
    scale_row = lax.rsqrt(jnp.mean(state * state, axis=-1, keepdims=True) + EPS)
    return (state * scale_row * gain_row).astype(jnp.bfloat16)


def shards(
    q_pre,
    k_pre,
    v_pre,
    q_bias,
    k_bias,
    v_bias,
    segment_ids,
    lengths,
    page_table,
    w_out,
    residual,
    norm_gain,
    w_gate,
    w_up,
):
    me_req = lax.axis_index("req")
    groups_all = lax.axis_size("req")
    block_rows = q_pre.shape[0]
    kv_heads = k_pre.shape[1] // HD
    q_heads = q_pre.shape[1] // HD
    group_size = q_heads // kv_heads
    own_lens = lax.dynamic_index_in_dim(lengths, me_req, 0, keepdims=False)
    own_pages = lax.dynamic_index_in_dim(page_table, me_req, 0, keepdims=False)
    own_owner = own_pages // REQS
    starts = jnp.cumsum(own_lens) - own_lens
    offsets = jnp.arange(PAGE, dtype=jnp.int32)
    row_index = jnp.clip(starts[:, None] + offsets[None, :], 0, block_rows - 1)
    flat_index = row_index.reshape(-1)
    request_ids = me_req * REQS + jnp.arange(REQS, dtype=jnp.int32)[:, None]
    inside = (offsets[None, :] < own_lens[:, None]) & (
        jnp.take(segment_ids, flat_index).reshape(REQS, PAGE) == request_ids
    )
    keep_mask = inside[:, :, None, None]
    positions = offsets.astype(jnp.float32)

    def prepare(source, bias_row, head_count):
        picked = jnp.take(source, flat_index, axis=0).astype(jnp.float32) + bias_row
        return picked.reshape(REQS, PAGE, head_count, HD)

    query_req = jnp.where(
        keep_mask, rotate(prepare(q_pre, q_bias, q_heads), positions), 0.0
    ).astype(jnp.bfloat16)
    key_req = jnp.where(keep_mask, rotate(prepare(k_pre, k_bias, kv_heads), positions), 0.0).astype(
        jnp.bfloat16
    )
    value_req = jnp.where(keep_mask, prepare(v_pre, v_bias, kv_heads), 0.0).astype(jnp.bfloat16)
    to_owner = (own_owner[None, :] == jnp.arange(groups_all)[:, None]).astype(jnp.bfloat16)
    alive_rows = segment_ids >= 0
    req_idx = jnp.clip(segment_ids - me_req * REQS, 0, REQS - 1)
    req_hit = req_idx[:, None] == jnp.arange(REQS)[None, :]
    row_start = jnp.sum(jnp.where(req_hit, starts[None, :], 0), axis=1)
    row_pos = jnp.clip(jnp.arange(block_rows, dtype=jnp.int32) - row_start, 0, PAGE - 1)
    hits = (
        page_table[None, :, :] == (me_req * REQS + jnp.arange(REQS, dtype=jnp.int32))[:, None, None]
    )
    page_select = jnp.sum(hits.astype(jnp.int32), axis=2).astype(jnp.bfloat16)
    q_send = jnp.einsum(
        "gj,jpc->gpc",
        to_owner,
        query_req.reshape(REQS, PAGE, q_heads * HD),
        preferred_element_type=jnp.float32,
    ).astype(jnp.bfloat16)
    k_send = jnp.einsum(
        "gj,jpc->gpc",
        to_owner,
        key_req.reshape(REQS, PAGE, kv_heads * HD),
        preferred_element_type=jnp.float32,
    ).astype(jnp.bfloat16)
    v_send = jnp.einsum(
        "gj,jpc->gpc",
        to_owner,
        value_req.reshape(REQS, PAGE, kv_heads * HD),
        preferred_element_type=jnp.float32,
    ).astype(jnp.bfloat16)
    q_in, k_in, v_in = (
        lax.all_to_all(q_send, "req", split_axis=0, concat_axis=0, tiled=True),
        lax.all_to_all(k_send, "req", split_axis=0, concat_axis=0, tiled=True),
        lax.all_to_all(v_send, "req", split_axis=0, concat_axis=0, tiled=True),
    )
    in_len = jnp.sum(jnp.where(page_table // REQS == me_req, lengths, 0), axis=1)
    q_groups = q_in.reshape(groups_all, PAGE, kv_heads, group_size, HD)
    k_groups = k_in.reshape(groups_all, PAGE, kv_heads, HD)
    v_groups = v_in.reshape(groups_all, PAGE, kv_heads, HD)
    pages_in = jnp.concatenate([k_groups, v_groups], axis=-1).transpose(0, 2, 1, 3)
    attended = attend(q_groups, k_groups, v_groups, in_len)
    returned = lax.all_to_all(
        attended.reshape(groups_all, PAGE, q_heads * HD),
        "req",
        split_axis=0,
        concat_axis=0,
        tiled=True,
    )
    row_group = jnp.sum(jnp.where(req_hit, own_owner[None, :], 0), axis=1)
    source_rows = jnp.take(
        returned.reshape(groups_all * PAGE, q_heads * HD), row_group * PAGE + row_pos, axis=0
    )
    cache_out = jnp.einsum(
        "ls,shpc->lhpc", page_select, pages_in, preferred_element_type=jnp.float32
    ).astype(jnp.bfloat16)
    attn_rows = jnp.where(alive_rows[:, None], source_rows, jnp.zeros((), jnp.bfloat16))
    summed = lax.psum(
        jnp.dot(attn_rows, w_out, preferred_element_type=jnp.float32).astype(jnp.bfloat16), "mp"
    ).astype(jnp.float32)
    normed = normalize(residual, summed, norm_gain)
    gate_acc = jnp.dot(
        normed,
        lax.all_gather(w_gate, "req", axis=0, tiled=True),
        preferred_element_type=jnp.float32,
    )
    up_acc = jnp.dot(
        normed, lax.all_gather(w_up, "req", axis=0, tiled=True), preferred_element_type=jnp.float32
    )
    hidden = (jax.nn.silu(gate_acc) * up_acc).astype(jnp.bfloat16)
    return (hidden, cache_out)


def solution(mesh):
    in_specs = (
        P("req", "mp"),
        P("req", "mp"),
        P("req", "mp"),
        P("mp"),
        P("mp"),
        P("mp"),
        P("req"),
        P(),
        P(),
        P("mp", None),
        P("req", None),
        P(),
        P("req", "mp"),
        P("req", "mp"),
    )
    out_specs = (P("req", "mp"), P("req", "mp", None, None))
    return jax.shard_map(shards, mesh=mesh, in_specs=in_specs, out_specs=out_specs, check_vma=False)
```

profile of v0, /device:TPU:1, one launch (start us, length us, event | category | flops | bytes accessed | tf_op | source)
XLA Modules:
  0.0 290.8 jit_solution(10564905103255792273)
XLA Ops:
  8.0 0.9 fusion.29
  9.0 0.1 copy.96
  9.1 0.2 reduce-window.4
  9.3 0.1 add_clamp_fusion
  9.4 0.4 copy-done.14
  9.8 3.6 %gather_fusion = s32[512]{0:T(512)S(1)} fusion(s32[512]{0:T(512)} %param.22, s32[1024]{0:T(1024)S(1)} %pad_clamp_fusion.2), kind=kCustom, calls=%fused_computation.2 | custom fusion | bytes 6144 | tf_op jit(solution)/shard_map/jit(_take)/gather | solution.py:89
  13.4 1.9 gather_fusion.1
  15.3 0.2 copy.78
  15.5 0.1 gather.22
  15.6 0.2 multiply_cosine_fusion
  15.8 0.1 fusion.35
  15.9 0.5 convert_add_fusion.1
  16.4 0.2 multiply_subtract_fusion
  16.6 0.3 pad_maximum_fusion
  17.0 0.1 fusion.10
  17.1 0.2 copy.80
  17.3 0.7 convolution_convert_fusion.2
  18.1 1.5 copy.81
  19.6 8.6 %all-to-all-start.2 = ((bf16[16,128,384]{2,1,0:T(8,128)(2,1)}), bf16[16,128,384]{2,1,0:T(8,128)(2,1)S(1)}, u32[]{:S(2)}, u32[]{:S(2)}) async-start(bf16[16,128,384]{2,1,0:T(8,128)(2,1)} %copy.81), calls=%async_computation.2 | async-start | bytes 3145728 | tf_op jit(solution)/shard_map/all_to_all | solution.py:134
  28.2 0.1 compare_select_fusion.2
  28.3 0.1 compare_and_fusion
  28.4 0.1 copy.74
  28.5 0.1 copy.76
  28.6 0.1 copy.70
  28.8 1.3 gather_fusion.4
  30.1 0.1 convert_add_fusion.2
  30.3 0.1 fusion.52
  30.4 0.4 subtract_bitcast_fusion
  30.8 0.6 convolution_convert_fusion.3
  31.4 0.9 copy.77
  32.4 1.3 gather_fusion.3
  33.8 0.1 convert_add_fusion.3
  33.9 0.6 convolution_convert_fusion.4
  34.5 16.6 %all-to-all-done.2 = bf16[16,128,384]{2,1,0:T(8,128)(2,1)S(1)} async-done(((bf16[16,128,384]{2,1,0:T(8,128)(2,1)}), bf16[16,128,384]{2,1,0:T(8,128)(2,1)S(1)}, u32[]{:S(2)}, u32[]{:S(2)}) %all-to-all-start.2) | async-done | bytes 1572896 | tf_op jit(solution)/shard_map/all_to_all | solution.py:134
  51.1 4.6 %all-to-all-start.1 = ((bf16[16,128,128]{2,1,0:T(8,128)(2,1)}), bf16[16,128,128]{2,1,0:T(8,128)(2,1)S(1)}, u32[]{:S(2)}, u32[]{:S(2)}) async-start(bf16[16,128,128]{2,1,0:T(8,128)(2,1)} %copy.77), calls=%async_computation.1 | async-start | bytes 1048576 | tf_op jit(solution)/shard_map/all_to_all | solution.py:135
  55.7 0.9 copy.72
  56.6 0.1 iota_compare_fusion.1
  56.7 0.3 broadcast_and_fusion
  57.1 1.7 copy.82
  58.7 7.1 %all-to-all-done.1 = bf16[16,128,128]{2,1,0:T(8,128)(2,1)S(1)} async-done(((bf16[16,128,128]{2,1,0:T(8,128)(2,1)}), bf16[16,128,128]{2,1,0:T(8,128)(2,1)S(1)}, u32[]{:S(2)}, u32[]{:S(2)}) %all-to-all-start.1) | async-done | bytes 524320 | tf_op jit(solution)/shard_map/all_to_all | solution.py:135
  65.8 4.2 %all-to-all-start = ((bf16[16,128,128]{2,1,0:T(8,128)(2,1)}), bf16[16,128,128]{2,1,0:T(8,128)(2,1)}, u32[]{:S(2)}, u32[]{:S(2)}) async-start(bf16[16,128,128]{2,1,0:T(8,128)(2,1)} %copy.72), calls=%async_computation | async-start | bytes 1048576 | tf_op jit(solution)/shard_map/all_to_all | solution.py:136
  70.1 2.2 fusion
  72.3 0.9 fusion.3
  73.2 6.2 %all-to-all-done = bf16[16,128,128]{2,1,0:T(8,128)(2,1)} async-done(((bf16[16,128,128]{2,1,0:T(8,128)(2,1)}), bf16[16,128,128]{2,1,0:T(8,128)(2,1)}, u32[]{:S(2)}, u32[]{:S(2)}) %all-to-all-start) | async-done | bytes 524320 | tf_op jit(solution)/shard_map/all_to_all | solution.py:136
  79.4 3.3 %convolution_convert_fusion.1 = bf16[16,128,3,128]{3,1,2,0:T(8,128)(2,1)} fusion(f32[16,128,128,3]{2,1,3,0:T(8,128)S(1)} %get-tuple-element.24, f32[16,3,128]{2,1,0:T(4,128)S(1)} %broadcast_select_fusion, f32[16,3,128]{2,1,0:T(4,128)S(1)} %get-tuple-element.23, pred[16,128,128]{1,2,0:T(8,128)(4,1)S(1)} %broadcast_and_fusion, ...), kind=kOutput, calls=%fused_computation.17 | convolution fusion | flops 206831616 | bytes 5556224 | tf_op jit(solution)/shard_map/shgqk,skhe->sqhge/dot_general | solution.py:46
  82.7 4.0 %all-to-all-start.3 = ((bf16[16,128,384]{1,2,0:T(8,128)(2,1)}), bf16[16,128,384]{1,2,0:T(8,128)(2,1)S(1)}, u32[]{:S(2)}, u32[]{:S(2)}) async-start(bf16[16,128,384]{1,2,0:T(8,128)(2,1)} %bitcast.106), calls=%async_computation.3 | async-start | bytes 3145728 | tf_op jit(solution)/shard_map/all_to_all | solution.py:144
  86.8 0.1 select_reduce_fusion
  87.0 0.5 compare_and_fusion.2
  87.5 18.7 %all-to-all-done.3 = bf16[16,128,384]{1,2,0:T(8,128)(2,1)S(1)} async-done(((bf16[16,128,384]{1,2,0:T(8,128)(2,1)}), bf16[16,128,384]{1,2,0:T(8,128)(2,1)S(1)}, u32[]{:S(2)}, u32[]{:S(2)}) %all-to-all-start.3) | async-done | bytes 1572896 | tf_op jit(solution)/shard_map/all_to_all | solution.py:144
  106.2 0.9 copy.86
  107.1 1.9 gather_fusion.2
  109.1 6.9 %convolution_convert_fusion = bf16[512,5120]{1,0:T(8,128)(2,1)} fusion(bf16[384,5120]{1,0:T(8,128)(2,1)} %param.25, bf16[512,384]{1,0:T(8,128)(2,1)S(1)} %gather_fusion.2, pred[512]{0:T(512)(128)(4,1)S(1)} %copy-done.12, pred[512]{0:T(512)(128)(4,1)S(1)} %broadcast_compare_fusion), kind=kOutput, calls=%fused_computation.8 | convolution fusion | flops 2016280576 | bytes 9569280 | tf_op jit(solution)/shard_map/dot_general | solution.py:160
  116.1 0.5 all-gather.3.cloned.1.call-update
  116.6 0.5 all-gather.5.cloned.1.call-update
  117.2 0.1 convert_reduce_fusion
  117.3 0.3 copy.110
  117.6 1.4 copy.109
  119.0 0.3 fusion.7
  119.3 0.7 copy.89
  120.0 74.5 %all-reduce.2.cloned.1.call-done = bf16[512,5120]{1,0:T(8,128)(2,1)} async-done(((bf16[512,5120]{1,0:T(8,128)(2,1)}), bf16[512,5120]{1,0:T(8,128)(2,1)}) %all-reduce.2.cloned.1.call-update) | async-done | bytes 5242896 | tf_op jit(solution)/shard_map/psum | solution.py:159
  194.5 5.8 %multiply_reduce_fusion = f32[512]{0:T(512)S(1)} fusion(bf16[512,5120]{1,0:T(8,128)(2,1)} %all-reduce.2.cloned.1.call-done, bf16[512,5120]{1,0:T(8,128)(2,1)} %param.26), kind=kLoop, calls=%fused_computation.6 | loop fusion | flops 13106688 | bytes 10487808 | tf_op jit(solution)/shard_map/reduce_sum | solution.py:54
  200.4 12.1 %fusion.51 = f32[512,864]{0,1:T(8,128)S(1)} fusion(bf16[5120,864]{1,0:T(8,128)(2,1)} %all-gather.3.cloned.1.call-done, bf16[512,5120]{1,0:T(8,128)(2,1)} %all-reduce.2.cloned.1.call-done, bf16[512,5120]{1,0:T(8,128)(2,1)} %param.26, f32[5120]{0:T(1024)S(1)} %copy-done.13, f32[512]{0:T(512)S(1)} %add_rsqrt_fusion), kind=kOutput, calls=%fused_computation.124 | convolution fusion | flops 4545576960 | bytes 21125120 | tf_op jit(solution)/shard_map/dot_general | solution.py:163
  212.5 58.1 %all-gather.5.cloned.1.call-done = bf16[5120,864]{1,0:T(8,128)(2,1)} async-done(((bf16[320,864]{1,0:T(8,128)(2,1)}), bf16[5120,864]{1,0:T(8,128)(2,1)}) %all-gather.5.cloned.1.call-update) | async-done | bytes 8847376 | tf_op jit(solution)/shard_map/all_gather | solution.py:169
  270.6 12.8 %multiply_convert_fusion.1 = bf16[512,864]{0,1:T(8,128)(2,1)} fusion(f32[512,864]{0,1:T(8,128)S(1)} %fusion.51, bf16[5120,864]{1,0:T(8,128)(2,1)} %all-gather.5.cloned.1.call-done, bf16[512,5120]{1,0:T(8,128)(2,1)} %all-reduce.2.cloned.1.call-done, bf16[512,5120]{1,0:T(8,128)(2,1)} %param.26, f32[5120]{0:T(1024)S(1)} %copy-done.13, f32[512]{0:T(512)S(1)} %add_rsqrt_fusion), kind=kOutput, calls=%fused_computation.16 | convolution fusion | flops 4548231168 | bytes 22009856 | tf_op jit(solution)/shard_map/dot_general | solution.py:168
  (54 shorter events, 0.5 us)
Async XLA Ops:
  8.0 5.4 %copy-start = (bf16[512,384]{1,0:T(8,128)(2,1)S(1)}, bf16[512,384]{1,0:T(8,128)(2,1)}, u32[]{:S(2)}) copy-start(bf16[512,384]{1,0:T(8,128)(2,1)} %param.16) | copy-start | bytes 1179652
  9.3 0.5 copy-start.14
  9.8 6.2 %copy-start.9 = (f32[384]{0:T(512)S(1)}, f32[384]{0:T(512)}, u32[]{:S(2)}) copy-start(f32[384]{0:T(512)} %param.19) | copy-start | bytes 4612
  18.1 10.7 %copy-start.3 = (bf16[512,128]{1,0:T(8,128)(2,1)S(1)}, bf16[512,128]{1,0:T(8,128)(2,1)}, u32[]{:S(2)}) copy-start(bf16[512,128]{1,0:T(8,128)(2,1)} %param.17) | copy-start | bytes 393220
  18.1 12.0 %copy-start.10 = (f32[128]{0:T(128)S(1)}, f32[128]{0:T(128)}, u32[]{:S(2)}) copy-start(f32[128]{0:T(128)} %param.20) | copy-start | bytes 1540
  19.6 31.5 %all-to-all-start.2 = ((bf16[16,128,384]{2,1,0:T(8,128)(2,1)}), bf16[16,128,384]{2,1,0:T(8,128)(2,1)S(1)}, u32[]{:S(2)}, u32[]{:S(2)}) async-start(bf16[16,128,384]{2,1,0:T(8,128)(2,1)} %copy.81), calls=%async_computation.2 | async-start | bytes 3145728 | tf_op jit(solution)/shard_map/all_to_all | solution.py:134
  28.2 4.2 %copy-start.4 = (bf16[512,128]{1,0:T(8,128)(2,1)S(1)}, bf16[512,128]{1,0:T(8,128)(2,1)}, u32[]{:S(2)}) copy-start(bf16[512,128]{1,0:T(8,128)(2,1)} %param.18) | copy-start | bytes 393220
  28.7 5.0 %copy-start.7 = (s32[16,4]{0,1:T(4,128)S(1)}, s32[16,4]{0,1:T(4,128)}, u32[]{:S(2)}) copy-start(s32[16,4]{0,1:T(4,128)} %param.24) | copy-start | bytes 772
  28.8 5.0 %copy-start.8 = (s32[16,4]{0,1:T(4,128)S(1)}, s32[16,4]{0,1:T(4,128)}, u32[]{:S(2)}) copy-start(s32[16,4]{0,1:T(4,128)} %param.23) | copy-start | bytes 772
  28.8 5.0 %copy-start.11 = (f32[128]{0:T(128)S(1)}, f32[128]{0:T(128)}, u32[]{:S(2)}) copy-start(f32[128]{0:T(128)} %param.21) | copy-start | bytes 1540
  51.1 14.7 %all-to-all-start.1 = ((bf16[16,128,128]{2,1,0:T(8,128)(2,1)}), bf16[16,128,128]{2,1,0:T(8,128)(2,1)S(1)}, u32[]{:S(2)}, u32[]{:S(2)}) async-start(bf16[16,128,128]{2,1,0:T(8,128)(2,1)} %copy.77), calls=%async_computation.1 | async-start | bytes 1048576 | tf_op jit(solution)/shard_map/all_to_all | solution.py:135
  65.8 4.2 %copy-start.5 = (bf16[16,128,128]{2,1,0:T(8,128)(2,1)}, bf16[16,128,128]{2,1,0:T(8,128)(2,1)S(1)}, u32[]{:S(2)}) copy-start(bf16[16,128,128]{2,1,0:T(8,128)(2,1)S(1)} %all-to-all-done.1) | copy-start | bytes 1572868
  65.8 13.6 %all-to-all-start = ((bf16[16,128,128]{2,1,0:T(8,128)(2,1)}), bf16[16,128,128]{2,1,0:T(8,128)(2,1)}, u32[]{:S(2)}, u32[]{:S(2)}) async-start(bf16[16,128,128]{2,1,0:T(8,128)(2,1)} %copy.72), calls=%async_computation | async-start | bytes 1048576 | tf_op jit(solution)/shard_map/all_to_all | solution.py:136
  82.7 4.1 %copy-start.15 = (s32[4,1]{0,1:T(1,128)S(1)}, s32[4,1]{0,1:T(1,128)}, u32[]{:S(2)}) copy-start(s32[4,1]{0,1:T(1,128)} %copy-done.14) | copy-start | bytes 52
  82.7 4.1 %copy-start.2 = (s32[512]{0:T(512)S(1)}, s32[512]{0:T(512)}, u32[]{:S(2)}) copy-start(s32[512]{0:T(512)} %param.22) | copy-start | bytes 6148
  82.7 23.5 %all-to-all-start.3 = ((bf16[16,128,384]{1,2,0:T(8,128)(2,1)}), bf16[16,128,384]{1,2,0:T(8,128)(2,1)S(1)}, u32[]{:S(2)}, u32[]{:S(2)}) async-start(bf16[16,128,384]{1,2,0:T(8,128)(2,1)} %bitcast.106), calls=%async_computation.3 | async-start | bytes 3145728 | tf_op jit(solution)/shard_map/all_to_all | solution.py:144
  86.7 107.8 %all-reduce.2.cloned.1.call-start = ((), (), s32[]{:S(2)}) async-start(), calls=%async_computation.4 | async-start | bytes 10485760 | tf_op jit(solution)/shard_map/psum | solution.py:159
  107.1 2.0 copy-start.12
  116.0 1.3 copy-start.6
  116.0 84.4 %all-gather.3.cloned.1.call-start = ((), (), s32[]{:S(2)}) async-start(), calls=%async_computation.5 | async-start | bytes 9748480 | tf_op jit(solution)/shard_map/all_gather | solution.py:165
  116.6 154.0 %all-gather.5.cloned.1.call-start = ((), (), s32[]{:S(2)}) async-start(), calls=%async_computation.6 | async-start | bytes 9748480 | tf_op jit(solution)/shard_map/all_gather | solution.py:169
  120.0 80.4 %copy-start.13 = (f32[5120]{0:T(1024)S(1)}, f32[5120]{0:T(1024)}, u32[]{:S(2)}) copy-start(f32[5120]{0:T(1024)} %param.27) | copy-start | bytes 61444
  270.6 12.8 %copy-start.1 = (bf16[512,384]{1,0:T(8,128)(2,1)S(1)}, bf16[512,384]{1,0:T(8,128)(2,1)}, u32[]{:S(2)}) copy-start(bf16[512,384]{1,0:T(8,128)(2,1)} %param.16) | copy-start | bytes 1179652
Sparse Core Ops, SparseCore 0:
  116.1 78.3 all-reduce.1
Sparse Core Ops, SparseCore 1:
  118.6 75.8 all-gather.2
  196.5 74.0 all-gather.4
where the time goes:
time: 291 us
  waiting for transfers between devices  182 us (63%)
  matrix products  39.5 us (14%)
  starting transfers between devices  21.5 us (7%)
  local copies, waits for them, and re-layouts  20.2 us (7%)
  between operations  16 us (5%)
  other arithmetic  11.3 us (4%)
    psum x1, waiting for transfers between devices, shards(): lax.psum(jnp.dot(attn_rows, w_out, preferred_element_type=jnp.float32).as...  74.5 us
    all_gather x1, waiting for transfers between devices, shards(): lax.all_gather(w_up, 'req', axis=0, tiled=True)  58.1 us
    all_to_all x1, waiting for transfers between devices, shards(): lax.all_to_all(attended.reshape(groups_all, PAGE, q_heads * HD), 'req', s...  18.7 us
    all_to_all x1, waiting for transfers between devices, shards(): lax.all_to_all(q_send, 'req', split_axis=0, concat_axis=0, tiled=True)  16.6 us
    dot_general x1, matrix products, shards(): jnp.dot(normed, lax.all_gather(w_up, 'req', axis=0, tiled=True), preferre...  12.8 us
    dot_general x1, matrix products, shards(): jnp.dot(normed, lax.all_gather(w_gate, 'req', axis=0, tiled=True), prefer...  12.1 us
    all_to_all x1, starting transfers between devices, shards(): lax.all_to_all(q_send, 'req', split_axis=0, concat_axis=0, tiled=True)  8.6 us
    all_to_all x1, waiting for transfers between devices, shards(): lax.all_to_all(k_send, 'req', split_axis=0, concat_axis=0, tiled=True)  7.09 us
  transfers between devices with their start and end apart: 7, of which 6 were waited for; matrix products, arithmetic and copies ran while one was open for 12% of the time, Pallas kernels for 0%

commit v1 on v0

--- a/solution.py
+++ b/solution.py
@@ -166,7 +166,11 @@
         preferred_element_type=jnp.float32,
     )
     up_acc = jnp.dot(
-        normed, lax.all_gather(w_up, "req", axis=0, tiled=True), preferred_element_type=jnp.float32
+        normed,
+        jnp.concatenate(
+            lax.all_to_all(jnp.stack([w_up] * lax.axis_size("req")), "req", 0, 0), axis=0
+        ),
+        preferred_element_type=jnp.float32,
     )
     hidden = (jax.nn.silu(gate_acc) * up_acc).astype(jnp.bfloat16)
     return (hidden, cache_out)

time: 291 us -> 338 us (1.16)
  waiting for transfers between devices: 182 us -> 214 us
  starting transfers between devices: 21.5 us -> 27.9 us
  local copies, waits for them, and re-layouts: 20.2 us -> 25.5 us
    all_gather x1, waiting for transfers between devices: 0.02 us -> 101 us  [shards(): lax.all_gather(w_gate, 'req', axis=0, tiled=True)]
    all_gather x1 -> x0, waiting for transfers between devices: 58.1 us -> none  [shards(): lax.all_gather(w_up, 'req', axis=0, tiled=True)]
    psum x1, waiting for transfers between devices: 74.5 us -> 64 us  [shards(): lax.psum(jnp.dot(attn_rows, w_out, preferred_element_type=jnp.float32).as...]
    all_to_all x0 -> x1, starting transfers between devices: none -> 6.24 us  [shards(): lax.all_to_all(jnp.stack([w_up] * lax.axis_size('req')), 'req', 0, 0)]
    another operation x0 -> x1, local copies, waits for them, and re-layouts: none -> 4.89 us  [shards(): jnp.stack([w_up] * lax.axis_size('req'))]
where the time goes in v1:
time: 338 us; the launch traced here: 335 us
  waiting for transfers between devices  214 us (63%)
  matrix products  39.6 us (12%)
  starting transfers between devices  27.9 us (8%)
  local copies, waits for them, and re-layouts  25.5 us (8%)
  between operations  16 us (5%)
  other arithmetic  11.3 us (3%)
    all_gather x1, waiting for transfers between devices, shards(): lax.all_gather(w_gate, 'req', axis=0, tiled=True)  101 us
    psum x1, waiting for transfers between devices, shards(): lax.psum(jnp.dot(attn_rows, w_out, preferred_element_type=jnp.float32).as...  64 us
    all_to_all x1, waiting for transfers between devices, shards(): lax.all_to_all(attended.reshape(groups_all, PAGE, q_heads * HD), 'req', s...  18.7 us
    all_to_all x1, waiting for transfers between devices, shards(): lax.all_to_all(q_send, 'req', split_axis=0, concat_axis=0, tiled=True)  16.6 us
    dot_general x1, matrix products, shards(): jnp.dot(normed, jnp.concatenate(lax.all_to_all(jnp.stack([w_up] * lax.axi...  12.8 us
    dot_general x1, matrix products, shards(): jnp.dot(normed, lax.all_gather(w_gate, 'req', axis=0, tiled=True), prefer...  12.1 us
    all_to_all x1, starting transfers between devices, shards(): lax.all_to_all(q_send, 'req', split_axis=0, concat_axis=0, tiled=True)  8.73 us
    all_to_all x1, waiting for transfers between devices, shards(): lax.all_to_all(k_send, 'req', split_axis=0, concat_axis=0, tiled=True)  7.09 us
  transfers between devices with their start and end apart: 7, of which 6 were waited for; matrix products, arithmetic and copies ran while one was open for 12% of the time, Pallas kernels for 0%

profile of v1, /device:TPU:1, one launch (start us, length us, event | category | flops | bytes accessed | tf_op | source)
XLA Modules:
  0.0 334.6 jit_solution(15420712958500936189)
XLA Ops:
  8.1 0.9 fusion.29
  9.0 0.1 copy.96
  9.1 0.2 reduce-window.4
  9.3 0.1 add_clamp_fusion
  9.4 0.4 copy-done.15
  9.8 3.6 %gather_fusion = s32[512]{0:T(512)S(1)} fusion(s32[512]{0:T(512)} %param.22, s32[1024]{0:T(1024)S(1)} %pad_clamp_fusion.2), kind=kCustom, calls=%fused_computation.2 | custom fusion | bytes 6144 | tf_op jit(solution)/shard_map/jit(_take)/gather | solution.py:89
  13.4 1.9 gather_fusion.1
  15.4 0.2 copy.78
  15.6 0.1 gather.22
  15.7 0.2 multiply_cosine_fusion
  15.9 0.1 fusion.35
  15.9 0.5 convert_add_fusion.1
  16.4 0.2 multiply_subtract_fusion
  16.6 0.3 pad_maximum_fusion
  17.0 0.1 fusion.10
  17.1 0.2 copy.80
  17.3 0.7 convolution_convert_fusion.2
  18.1 1.5 copy.81
  19.6 8.7 %all-to-all-start.2 = ((bf16[16,128,384]{2,1,0:T(8,128)(2,1)}), bf16[16,128,384]{2,1,0:T(8,128)(2,1)S(1)}, u32[]{:S(2)}, u32[]{:S(2)}) async-start(bf16[16,128,384]{2,1,0:T(8,128)(2,1)} %copy.81), calls=%async_computation.2 | async-start | bytes 3145728 | tf_op jit(solution)/shard_map/all_to_all | solution.py:134
  28.4 0.1 compare_and_fusion
  28.5 0.1 copy.70
  28.7 0.1 copy.74
  28.7 0.1 copy.76
  28.9 1.3 gather_fusion.4
  30.3 1.3 gather_fusion.3
  31.6 0.1 convert_add_fusion.2
  31.8 0.1 fusion.52
  31.9 0.4 subtract_bitcast_fusion
  32.3 0.6 convolution_convert_fusion.3
  32.9 0.9 copy.77
  33.9 0.1 convert_add_fusion.3
  34.0 0.6 convolution_convert_fusion.4
  34.6 16.6 %all-to-all-done.2 = bf16[16,128,384]{2,1,0:T(8,128)(2,1)S(1)} async-done(((bf16[16,128,384]{2,1,0:T(8,128)(2,1)}), bf16[16,128,384]{2,1,0:T(8,128)(2,1)S(1)}, u32[]{:S(2)}, u32[]{:S(2)}) %all-to-all-start.2) | async-done | bytes 1572896 | tf_op jit(solution)/shard_map/all_to_all | solution.py:134
  51.2 4.6 %all-to-all-start.1 = ((bf16[16,128,128]{2,1,0:T(8,128)(2,1)}), bf16[16,128,128]{2,1,0:T(8,128)(2,1)S(1)}, u32[]{:S(2)}, u32[]{:S(2)}) async-start(bf16[16,128,128]{2,1,0:T(8,128)(2,1)} %copy.77), calls=%async_computation.1 | async-start | bytes 1048576 | tf_op jit(solution)/shard_map/all_to_all | solution.py:135
  55.8 0.9 copy.72
  56.8 0.3 broadcast_and_fusion
  57.2 1.7 copy.82
  58.8 7.1 %all-to-all-done.1 = bf16[16,128,128]{2,1,0:T(8,128)(2,1)S(1)} async-done(((bf16[16,128,128]{2,1,0:T(8,128)(2,1)}), bf16[16,128,128]{2,1,0:T(8,128)(2,1)S(1)}, u32[]{:S(2)}, u32[]{:S(2)}) %all-to-all-start.1) | async-done | bytes 524320 | tf_op jit(solution)/shard_map/all_to_all | solution.py:135
  65.9 4.2 %all-to-all-start = ((bf16[16,128,128]{2,1,0:T(8,128)(2,1)}), bf16[16,128,128]{2,1,0:T(8,128)(2,1)}, u32[]{:S(2)}, u32[]{:S(2)}) async-start(bf16[16,128,128]{2,1,0:T(8,128)(2,1)} %copy.72), calls=%async_computation | async-start | bytes 1048576 | tf_op jit(solution)/shard_map/all_to_all | solution.py:136
  70.2 2.2 fusion
  72.4 0.9 fusion.3
  73.3 6.2 %all-to-all-done = bf16[16,128,128]{2,1,0:T(8,128)(2,1)} async-done(((bf16[16,128,128]{2,1,0:T(8,128)(2,1)}), bf16[16,128,128]{2,1,0:T(8,128)(2,1)}, u32[]{:S(2)}, u32[]{:S(2)}) %all-to-all-start) | async-done | bytes 524320 | tf_op jit(solution)/shard_map/all_to_all | solution.py:136
  79.5 3.3 %convolution_convert_fusion.1 = bf16[16,128,3,128]{3,1,2,0:T(8,128)(2,1)} fusion(f32[16,128,128,3]{2,1,3,0:T(8,128)S(1)} %get-tuple-element.24, f32[16,3,128]{2,1,0:T(4,128)S(1)} %broadcast_select_fusion, f32[16,3,128]{2,1,0:T(4,128)S(1)} %get-tuple-element.23, pred[16,128,128]{1,2,0:T(8,128)(4,1)S(1)} %broadcast_and_fusion, ...), kind=kOutput, calls=%fused_computation.17 | convolution fusion | flops 206831616 | bytes 5556224 | tf_op jit(solution)/shard_map/shgqk,skhe->sqhge/dot_general | solution.py:46
  82.9 4.0 %all-to-all-start.3 = ((bf16[16,128,384]{1,2,0:T(8,128)(2,1)}), bf16[16,128,384]{1,2,0:T(8,128)(2,1)S(1)}, u32[]{:S(2)}, u32[]{:S(2)}) async-start(bf16[16,128,384]{1,2,0:T(8,128)(2,1)} %bitcast.107), calls=%async_computation.3 | async-start | bytes 3145728 | tf_op jit(solution)/shard_map/all_to_all | solution.py:144
  87.0 0.1 select_reduce_fusion
  87.1 0.5 compare_and_fusion.2
  87.7 18.7 %all-to-all-done.3 = bf16[16,128,384]{1,2,0:T(8,128)(2,1)S(1)} async-done(((bf16[16,128,384]{1,2,0:T(8,128)(2,1)}), bf16[16,128,384]{1,2,0:T(8,128)(2,1)S(1)}, u32[]{:S(2)}, u32[]{:S(2)}) %all-to-all-start.3) | async-done | bytes 1572896 | tf_op jit(solution)/shard_map/all_to_all | solution.py:144
  106.4 0.9 copy.86
  107.2 1.9 gather_fusion.2
  109.2 7.0 %convolution_convert_fusion = bf16[512,5120]{1,0:T(8,128)(2,1)} fusion(bf16[384,5120]{1,0:T(8,128)(2,1)} %param.25, bf16[512,384]{1,0:T(8,128)(2,1)S(1)} %gather_fusion.2, pred[512]{0:T(512)(128)(4,1)S(1)} %copy-done.13, pred[512]{0:T(512)(128)(4,1)S(1)} %broadcast_compare_fusion), kind=kOutput, calls=%fused_computation.8 | convolution fusion | flops 2016280576 | bytes 9569280 | tf_op jit(solution)/shard_map/dot_general | solution.py:160
  116.3 0.5 all-gather.2.cloned.1.call-update
  116.8 0.5 copy-done.7
  117.2 4.9 %stack.2 = bf16[16,320,864]{2,1,0:T(8,128)(2,1)} broadcast(bf16[320,864]{1,0:T(8,128)(2,1)S(1)} %copy-done.7), dimensions={1,2} | broadcast | bytes 9400320 | tf_op jit(solution)/shard_map/stack | solution.py:171
  122.1 6.2 %all-to-all-start.4 = ((bf16[16,320,864]{2,1,0:T(8,128)(2,1)}), bf16[16,320,864]{2,1,0:T(8,128)(2,1)}, u32[]{:S(2)}, u32[]{:S(2)}) async-start(bf16[16,320,864]{2,1,0:T(8,128)(2,1)} %stack.2), calls=%async_computation.4 | async-start | bytes 18350080 | tf_op jit(solution)/shard_map/all_to_all | solution.py:171
  128.4 0.1 convert_reduce_fusion
  128.5 1.4 copy.109
  129.9 0.3 copy.110
  130.2 0.3 fusion.7
  130.5 0.7 copy.89
  131.2 64.0 %all-reduce.2.cloned.1.call-done = bf16[512,5120]{1,0:T(8,128)(2,1)} async-done(((bf16[512,5120]{1,0:T(8,128)(2,1)}), bf16[512,5120]{1,0:T(8,128)(2,1)}) %all-reduce.2.cloned.1.call-update) | async-done | bytes 5242896 | tf_op jit(solution)/shard_map/psum | solution.py:159
  195.2 5.8 %multiply_reduce_fusion = f32[512]{0:T(512)S(1)} fusion(bf16[512,5120]{1,0:T(8,128)(2,1)} %all-reduce.2.cloned.1.call-done, bf16[512,5120]{1,0:T(8,128)(2,1)} %param.26), kind=kLoop, calls=%fused_computation.6 | loop fusion | flops 13106688 | bytes 10487808 | tf_op jit(solution)/shard_map/reduce_sum | solution.py:54
  201.0 101.2 %all-gather.2.cloned.1.call-done = bf16[5120,864]{1,0:T(8,128)(2,1)} async-done(((bf16[320,864]{1,0:T(8,128)(2,1)}), bf16[5120,864]{1,0:T(8,128)(2,1)}) %all-gather.2.cloned.1.call-update) | async-done | bytes 8847376 | tf_op jit(solution)/shard_map/all_gather | solution.py:165
  302.3 12.1 %fusion.51 = f32[512,864]{0,1:T(8,128)S(1)} fusion(bf16[5120,864]{1,0:T(8,128)(2,1)} %all-gather.2.cloned.1.call-done, bf16[512,5120]{1,0:T(8,128)(2,1)} %all-reduce.2.cloned.1.call-done, bf16[512,5120]{1,0:T(8,128)(2,1)} %param.26, f32[5120]{0:T(1024)S(1)} %copy-done.14, f32[512]{0:T(512)S(1)} %add_rsqrt_fusion), kind=kOutput, calls=%fused_computation.124 | convolution fusion | flops 4545576960 | bytes 21125120 | tf_op jit(solution)/shard_map/dot_general | solution.py:163
  314.3 12.8 %multiply_convert_fusion.1 = bf16[512,864]{0,1:T(8,128)(2,1)} fusion(f32[512,864]{0,1:T(8,128)S(1)} %fusion.51, bf16[5120,864]{1,0:T(8,128)(2,1)} %bitcast.31, bf16[512,5120]{1,0:T(8,128)(2,1)} %all-reduce.2.cloned.1.call-done, bf16[512,5120]{1,0:T(8,128)(2,1)} %param.26, f32[5120]{0:T(1024)S(1)} %copy-done.14, f32[512]{0:T(512)S(1)} %add_rsqrt_fusion), kind=kOutput, calls=%fused_computation.16 | convolution fusion | flops 4548231168 | bytes 22009856 | tf_op jit(solution)/shard_map/dot_general | solution.py:168
  (56 shorter events, 0.6 us)
Async XLA Ops:
  8.0 5.4 %copy-start = (bf16[512,384]{1,0:T(8,128)(2,1)S(1)}, bf16[512,384]{1,0:T(8,128)(2,1)}, u32[]{:S(2)}) copy-start(bf16[512,384]{1,0:T(8,128)(2,1)} %param.16) | copy-start | bytes 1179652
  9.3 0.5 copy-start.15
  9.8 6.2 %copy-start.10 = (f32[384]{0:T(512)S(1)}, f32[384]{0:T(512)}, u32[]{:S(2)}) copy-start(f32[384]{0:T(512)} %param.19) | copy-start | bytes 4612
  18.1 10.8 %copy-start.3 = (bf16[512,128]{1,0:T(8,128)(2,1)S(1)}, bf16[512,128]{1,0:T(8,128)(2,1)}, u32[]{:S(2)}) copy-start(bf16[512,128]{1,0:T(8,128)(2,1)} %param.17) | copy-start | bytes 393220
  18.1 12.2 %copy-start.4 = (bf16[512,128]{1,0:T(8,128)(2,1)S(1)}, bf16[512,128]{1,0:T(8,128)(2,1)}, u32[]{:S(2)}) copy-start(bf16[512,128]{1,0:T(8,128)(2,1)} %param.18) | copy-start | bytes 393220
  19.6 12.0 %copy-start.11 = (f32[128]{0:T(128)S(1)}, f32[128]{0:T(128)}, u32[]{:S(2)}) copy-start(f32[128]{0:T(128)} %param.20) | copy-start | bytes 1540
  19.6 31.6 %all-to-all-start.2 = ((bf16[16,128,384]{2,1,0:T(8,128)(2,1)}), bf16[16,128,384]{2,1,0:T(8,128)(2,1)S(1)}, u32[]{:S(2)}, u32[]{:S(2)}) async-start(bf16[16,128,384]{2,1,0:T(8,128)(2,1)} %copy.81), calls=%async_computation.2 | async-start | bytes 3145728 | tf_op jit(solution)/shard_map/all_to_all | solution.py:134
  28.9 5.0 %copy-start.8 = (s32[16,4]{0,1:T(4,128)S(1)}, s32[16,4]{0,1:T(4,128)}, u32[]{:S(2)}) copy-start(s32[16,4]{0,1:T(4,128)} %param.24) | copy-start | bytes 772
  28.9 5.0 %copy-start.9 = (s32[16,4]{0,1:T(4,128)S(1)}, s32[16,4]{0,1:T(4,128)}, u32[]{:S(2)}) copy-start(s32[16,4]{0,1:T(4,128)} %param.23) | copy-start | bytes 772
  28.9 5.0 %copy-start.12 = (f32[128]{0:T(128)S(1)}, f32[128]{0:T(128)}, u32[]{:S(2)}) copy-start(f32[128]{0:T(128)} %param.21) | copy-start | bytes 1540
  51.2 14.7 %all-to-all-start.1 = ((bf16[16,128,128]{2,1,0:T(8,128)(2,1)}), bf16[16,128,128]{2,1,0:T(8,128)(2,1)S(1)}, u32[]{:S(2)}, u32[]{:S(2)}) async-start(bf16[16,128,128]{2,1,0:T(8,128)(2,1)} %copy.77), calls=%async_computation.1 | async-start | bytes 1048576 | tf_op jit(solution)/shard_map/all_to_all | solution.py:135
  65.9 4.2 %copy-start.5 = (bf16[16,128,128]{2,1,0:T(8,128)(2,1)}, bf16[16,128,128]{2,1,0:T(8,128)(2,1)S(1)}, u32[]{:S(2)}) copy-start(bf16[16,128,128]{2,1,0:T(8,128)(2,1)S(1)} %all-to-all-done.1) | copy-start | bytes 1572868
  65.9 13.6 %all-to-all-start = ((bf16[16,128,128]{2,1,0:T(8,128)(2,1)}), bf16[16,128,128]{2,1,0:T(8,128)(2,1)}, u32[]{:S(2)}, u32[]{:S(2)}) async-start(bf16[16,128,128]{2,1,0:T(8,128)(2,1)} %copy.72), calls=%async_computation | async-start | bytes 1048576 | tf_op jit(solution)/shard_map/all_to_all | solution.py:136
  82.9 4.1 %copy-start.16 = (s32[4,1]{0,1:T(1,128)S(1)}, s32[4,1]{0,1:T(1,128)}, u32[]{:S(2)}) copy-start(s32[4,1]{0,1:T(1,128)} %copy-done.15) | copy-start | bytes 52
  82.9 4.1 %copy-start.2 = (s32[512]{0:T(512)S(1)}, s32[512]{0:T(512)}, u32[]{:S(2)}) copy-start(s32[512]{0:T(512)} %param.22) | copy-start | bytes 6148
  82.9 23.5 %all-to-all-start.3 = ((bf16[16,128,384]{1,2,0:T(8,128)(2,1)}), bf16[16,128,384]{1,2,0:T(8,128)(2,1)S(1)}, u32[]{:S(2)}, u32[]{:S(2)}) async-start(bf16[16,128,384]{1,2,0:T(8,128)(2,1)} %bitcast.107), calls=%async_computation.3 | async-start | bytes 3145728 | tf_op jit(solution)/shard_map/all_to_all | solution.py:144
  86.9 108.3 %all-reduce.2.cloned.1.call-start = ((), (), s32[]{:S(2)}) async-start(), calls=%async_computation.5 | async-start | bytes 10485760 | tf_op jit(solution)/shard_map/psum | solution.py:159
  107.2 2.0 copy-start.13
  116.2 1.1 copy-start.7
  116.2 186.0 %all-gather.2.cloned.1.call-start = ((), (), s32[]{:S(2)}) async-start(), calls=%async_computation.6 | async-start | bytes 9748480 | tf_op jit(solution)/shard_map/all_gather | solution.py:165
  122.1 7.7 %copy-start.6 = (bf16[16,128,128]{2,1,0:T(8,128)(2,1)S(1)}, bf16[16,128,128]{2,1,0:T(8,128)(2,1)}, u32[]{:S(2)}) copy-start(bf16[16,128,128]{2,1,0:T(8,128)(2,1)} %copy-done.5) | copy-start | bytes 1572868
  122.1 192.2 %all-to-all-start.4 = ((bf16[16,320,864]{2,1,0:T(8,128)(2,1)}), bf16[16,320,864]{2,1,0:T(8,128)(2,1)}, u32[]{:S(2)}, u32[]{:S(2)}) async-start(bf16[16,320,864]{2,1,0:T(8,128)(2,1)} %stack.2), calls=%async_computation.4 | async-start | bytes 18350080 | tf_op jit(solution)/shard_map/all_to_all | solution.py:171
  131.2 171.0 %copy-start.14 = (f32[5120]{0:T(1024)S(1)}, f32[5120]{0:T(1024)}, u32[]{:S(2)}) copy-start(f32[5120]{0:T(1024)} %param.27) | copy-start | bytes 61444
  314.3 12.8 %copy-start.1 = (bf16[512,384]{1,0:T(8,128)(2,1)S(1)}, bf16[512,384]{1,0:T(8,128)(2,1)}, u32[]{:S(2)}) copy-start(bf16[512,384]{1,0:T(8,128)(2,1)} %param.16) | copy-start | bytes 1179652
Sparse Core Ops, SparseCore 0:
  116.3 78.8 all-reduce.1
Sparse Core Ops, SparseCore 1:
  118.8 183.4 all-gather.1
